TPU v7x, 256 devices: a whole 4x4x8 slice. The times are simulated.
256 devices in a mesh: lon: 16 (over x, y_lo, core), lat: 8 (over z), tm: 2 (over y_hi).
Axes of the slice: x: 4, y: 4 (y_hi: 2, y_lo: 2; y = y_hi * 2 + y_lo), z: 8, core: 2. Of those that a mesh axis runs over, the one named last changes fastest.
Arguments:
- snapshots: float32 [16, 8, 128, 2048], P('tm', None, 'lat', 'lon'), may hold values from -6 to 6
- basis: float32 [64, 8, 128, 2048], P(None, None, 'lat', 'lon'), may hold values from -6 to 6
Outputs:
- new_basis: float32 [64, 8, 128, 2048], P(None, None, 'lat', 'lon')
- coeffs: float32 [64, 16], P(None, 'tm')
All inputs are finite; a program needn't handle non-finite values.
Results may differ from a plain program's by a relative error of at most 0.00011.
Values sent between devices are 32-bit elements; how exact they have to be, the bound alone decides.
No kernel may reach another device: no remote copies, remote signals or barrier semaphores. Data moves between devices by JAX's collectives and lax.ppermute only.
A program may use at most 64 MiB of HBM per device.

v0:
```python
import math
import jax
import jax.numpy as jnp
from jax import lax
from jax.sharding import PartitionSpec as P

SMOOTH_RATE = 0.1
STEP_SIZE = 0.25


def with_halo(cells, sides, width, closed):
    for axis, dim in sides:
        count = lax.axis_size(axis)
        ends = count if closed else count - 1
        head = lax.slice_in_dim(cells, 0, width, axis=dim)
        tail = lax.slice_in_dim(cells, cells.shape[dim] - width, cells.shape[dim], axis=dim)
        cells = jnp.concatenate(
            [
                lax.ppermute(tail, axis, [(i, (i + 1) % count) for i in range(ends)]),
                cells,
                lax.ppermute(head, axis, [((i + 1) % count, i) for i in range(ends)]),
            ],
            axis=dim,
        )
    return cells


def product(left, right):
    return jnp.dot(left, right, precision=lax.Precision.HIGHEST, preferred_element_type=jnp.float32)


def laplace_step(extended):
    padded = jnp.pad(extended, ((0, 0), (1, 1), (0, 0), (0, 0)))
    center = extended[:, :, 1:-1, 1:-1]
    neighbours = padded[:, 2:, 1:-1, 1:-1] + padded[:, :-2, 1:-1, 1:-1]
    neighbours = neighbours + extended[:, :, 2:, 1:-1] + extended[:, :, :-2, 1:-1]
    neighbours = neighbours + extended[:, :, 1:-1, 2:] + extended[:, :, 1:-1, :-2]
    return center + SMOOTH_RATE * (neighbours - 6.0 * center)


def finish(grown, gram_matrix):
    factor = jnp.linalg.cholesky(gram_matrix)
    return jax.scipy.linalg.solve_triangular(factor, grown, lower=True)


def shards(snapshots, basis):
    snap_count, levels, rows_lat, cols_lon = snapshots.shape
    eof_count = basis.shape[0]
    total_cells = levels * rows_lat * cols_lon * lax.axis_size("lat") * lax.axis_size("lon")
    inv_root = 1.0 / math.sqrt(total_cells)
    smoothed = snapshots
    for sweep in range(3):
        lat_wide = with_halo(smoothed, (("lat", 2),), 1, False)
        extended = with_halo(lat_wide, (("lon", 3),), 1, True)
        smoothed = laplace_step(extended)
    flattened = smoothed.reshape(snap_count, -1)
    columns = basis.reshape(eof_count, -1)
    coeffs = lax.psum(product(columns, flattened.T), ("lon", "lat")) * inv_root
    update_term = STEP_SIZE * product(coeffs, flattened)
    grown = columns + lax.psum(update_term, "tm")
    gram_matrix = lax.psum(product(grown, grown.T), ("lon", "lat")) / total_cells
    new_basis = finish(grown, gram_matrix)
    return (new_basis.reshape(basis.shape), coeffs)


def solution(mesh):
    placed = (P("tm", None, "lat", "lon"), P(None, None, "lat", "lon"))
    return jax.shard_map(
        shards,
        mesh=mesh,
        in_specs=placed,
        out_specs=(P(None, None, "lat", "lon"), P(None, "tm")),
        check_vma=False,
    )
```

profile of v0, /device:TPU:16, one launch (start us, length us, event | category | flops | bytes accessed | tf_op | source)
XLA Modules:
  0.0 1095.1 jit_solution(14280274604795155072)
XLA Ops:
  7.2 1.2 copy.90
  8.4 1.3 collective-permute-start.1
  9.7 4.5 collective-permute-start
  14.3 3.5 copy.78
  17.8 2.7 copy.79
  20.5 2.6 copy.77
  23.1 6.9 pad_maximum_fusion
  30.0 2.0 copy-done.1
  32.0 3.9 collective-permute-start.3
  35.9 2.9 copy.81
  41.6 3.8 collective-permute-start.4
  45.5 1.3 collective-permute-start.5
  47.1 4.2 collective-permute-done.5
  52.0 1.5 collective-permute-start.7
  55.6 4.3 collective-permute-done.6
  62.4 4.8 collective-permute-start.8
  67.3 1.3 collective-permute-start.9
  68.8 4.3 collective-permute-done.9
  76.1 3.9 collective-permute-done.10
  82.5 1.3 copy-done
  83.8 5.3 fusion.7
  89.2 278.5 %psum.21 = f32[64,8]{0,1:T(8,128)S(1)} all-reduce(f32[64,8]{0,1:T(8,128)S(1)} %fusion.7), channel_id=1, replica_groups=mesh['lon'=16,'lat'=8,'tm'=2] {'lon','lat'}, use_global_device_ids=true, to_apply=%region_0.1 | all-reduce | flops 512 | bytes 4096 | tf_op jit(solution)/shard_map/psum | solution.py:58
  367.7 5.1 convolution_multiply_fusion
  372.8 112.3 %all-reduce.5.cloned.1.call-done = f32[64,16384]{1,0:T(8,128)} async-done(((f32[64,16384]{1,0:T(8,128)}), f32[64,16384]{1,0:T(8,128)}) %all-reduce.5.cloned.1.call-update) | async-done | bytes 4194320 | tf_op jit(solution)/shard_map/psum | solution.py:60
  485.1 14.0 %fusion.6 = f32[64,64]{0,1:T(8,128)S(1)} fusion(f32[64,16384]{1,0:T(8,128)} %all-reduce.5.cloned.1.call-done, f32[8,8,128,128]{3,2,1,0:T(8,128)} %bitcast.37), kind=kOutput, calls=%fused_computation.21 | convolution fusion | flops 806354944 | bytes 8404992 | tf_op jit(solution)/shard_map/dot_general | solution.py:29
  499.1 555.0 %psum.23 = f32[64,64]{0,1:T(8,128)S(1)} all-reduce(f32[64,64]{0,1:T(8,128)S(1)} %fusion.6), channel_id=1, replica_groups=mesh['lon'=16,'lat'=8,'tm'=2] {'lon','lat'}, use_global_device_ids=true, to_apply=%region_2.3 | all-reduce | flops 4096 | bytes 32768 | tf_op jit(solution)/shard_map/psum | solution.py:61
  1054.1 6.1 fusion.5
  1060.2 2.8 copy.121
  1063.1 5.8 cholesky.16
  1070.3 4.9 custom-call.7
  1075.2 8.4 fusion
  1083.6 4.4 copy.110
  (50 shorter events, 15.6 us)
Async XLA Ops:
  7.2 477.9 %all-reduce.5.cloned.1.call-start = ((), (), s32[]{:S(2)}) async-start(), calls=%async_computation | async-start | bytes 8388608 | tf_op jit(solution)/shard_map/psum | solution.py:60
  8.4 9.4 collective-permute-start.1
  9.7 10.7 collective-permute-start
  30.0 2.0 copy-start.1
  32.0 6.7 collective-permute-start.2
  32.0 7.2 collective-permute-start.3
  41.6 5.4 collective-permute-start.4
  45.5 5.8 collective-permute-start.5
  52.0 3.1 collective-permute-start.7
  54.0 6.0 collective-permute-start.6
  62.4 6.4 collective-permute-start.8
  67.3 5.9 collective-permute-start.9
  73.9 1.7 collective-permute-start.11
  74.5 5.5 collective-permute-start.10
  81.6 2.2 copy-start
  367.7 5.1 copy-start.2
Sparse Core Ops, SparseCore 0:
  372.9 112.1 all-reduce.4
where the time goes:
time: 1100 us
  blocking collectives  834 us (76%)
  waiting for transfers between devices  131 us (12%)
  matrix products  32.8 us (3%)
  other arithmetic  30.9 us (3%)
  local copies, waits for them, and re-layouts  29 us (3%)
  starting transfers between devices  23.6 us (2%)
  between operations  14.5 us (1%)
    psum x1, blocking collectives, shards(): lax.psum(product(grown, grown.T), ('lon', 'lat')) / total_cells  555 us
    psum x1, blocking collectives, shards(): coeffs = lax.psum(product(columns, flattened.T), ('lon', 'lat')) * inv_root  279 us
    psum x1, waiting for transfers between devices, shards(): grown = columns + lax.psum(update_term, 'tm')  112 us
    dot_general x3, matrix products, product(): jnp.dot(left, right, precision=lax.Precision.HIGHEST, preferred_element_t...  24.4 us
  transfers between devices with their start and end apart: 13, of which 9 were waited for; matrix products, arithmetic and copies ran while one was open for 1% of the time, Pallas kernels for 0%

commit v1 on v0

--- a/solution.py
+++ b/solution.py
@@ -1,3 +1,4 @@
+import functools
 import math
 import jax
 import jax.numpy as jnp
@@ -6,6 +7,13 @@
 
 SMOOTH_RATE = 0.1
 STEP_SIZE = 0.25
+
+
+def watch_face(vals, row_axis, axis_id):
+    return jax.lax.psum(jax.lax.psum(vals, axis_name=row_axis), axis_id)
+
+
+sizes_move = functools.partial(watch_face, row_axis="lon", axis_id="lat")
 
 
 def with_halo(cells, sides, width, closed):
@@ -55,7 +63,7 @@
         smoothed = laplace_step(extended)
     flattened = smoothed.reshape(snap_count, -1)
     columns = basis.reshape(eof_count, -1)
-    coeffs = lax.psum(product(columns, flattened.T), ("lon", "lat")) * inv_root
+    coeffs = sizes_move(product(columns, flattened.T)) * inv_root
     update_term = STEP_SIZE * product(coeffs, flattened)
     grown = columns + lax.psum(update_term, "tm")
     gram_matrix = lax.psum(product(grown, grown.T), ("lon", "lat")) / total_cells

time: 1100 us -> 873 us (0.79)
  blocking collectives: 834 us -> 599 us
    psum x1 -> x2, blocking collectives: 279 us -> 44.2 us  [watch_face(): return jax.lax.psum(jax.lax.psum(vals, axis_name=row_axis), axis_id)]
where the time goes in v1:
time: 873 us; the launch traced here: 865 us
  blocking collectives  599 us (69%)
  waiting for transfers between devices  135 us (15%)
  matrix products  32.8 us (4%)
  other arithmetic  31 us (4%)
  local copies, waits for them, and re-layouts  29 us (3%)
  starting transfers between devices  23.6 us (3%)
  between operations  14.5 us (2%)
    psum x1, blocking collectives, shards(): lax.psum(product(grown, grown.T), ('lon', 'lat')) / total_cells  555 us
    psum x1, waiting for transfers between devices, shards(): grown = columns + lax.psum(update_term, 'tm')  117 us
    psum x2, blocking collectives, watch_face(): return jax.lax.psum(jax.lax.psum(vals, axis_name=row_axis), axis_id)  44.2 us
    dot_general x3, matrix products, product(): jnp.dot(left, right, precision=lax.Precision.HIGHEST, preferred_element_t...  24.3 us
  transfers between devices with their start and end apart: 13, of which 9 were waited for; matrix products, arithmetic and copies ran while one was open for 1% of the time, Pallas kernels for 0%

profile of v1, /device:TPU:16, one launch (start us, length us, event | category | flops | bytes accessed | tf_op | source)
XLA Modules:
  0.0 865.1 jit_solution(14600010781492581711)
XLA Ops:
  8.4 1.3 collective-permute-start.1
  9.7 4.5 collective-permute-start
  14.3 3.5 copy.78
  17.8 2.7 copy.79
  20.5 2.6 copy.77
  23.1 6.9 pad_maximum_fusion
  30.0 2.0 copy-done.1
  32.0 3.9 collective-permute-start.3
  35.9 2.9 copy.81
  41.6 3.8 collective-permute-start.4
  45.5 1.3 collective-permute-start.5
  47.0 4.2 collective-permute-done.5
  52.0 1.5 collective-permute-start.7
  55.6 4.3 collective-permute-done.6
  62.4 4.8 collective-permute-start.8
  67.3 1.3 collective-permute-start.9
  68.8 4.3 collective-permute-done.9
  76.1 3.9 collective-permute-done.10
  82.5 1.3 copy-done
  83.8 5.3 fusion.7
  89.2 27.1 %psum.28 = f32[64,8]{0,1:T(8,128)S(1)} all-reduce(f32[64,8]{0,1:T(8,128)S(1)} %fusion.7), channel_id=1, replica_groups=mesh['lon'=16,'lat'=8,'tm'=2] {'lon'}, use_global_device_ids=true, to_apply=%region_0.1 | all-reduce | flops 512 | bytes 4096 | tf_op jit(solution)/shard_map/psum | solution.py:13
  116.3 17.1 %psum.29 = f32[64,8]{0,1:T(8,128)S(1)} all-reduce(f32[64,8]{0,1:T(8,128)S(1)} %psum.28), channel_id=1, replica_groups=mesh['lon'=16,'lat'=8,'tm'=2] {'lat'}, use_global_device_ids=true, to_apply=%region_1.2 | all-reduce | flops 512 | bytes 4096 | tf_op jit(solution)/shard_map/psum | solution.py:13
  133.4 5.1 convolution_multiply_fusion
  138.5 116.5 %all-reduce.5.cloned.1.call-done = f32[64,16384]{1,0:T(8,128)} async-done(((f32[64,16384]{1,0:T(8,128)}), f32[64,16384]{1,0:T(8,128)}) %all-reduce.5.cloned.1.call-update) | async-done | bytes 4194320 | tf_op jit(solution)/shard_map/psum | solution.py:68
  255.0 13.9 %fusion.6 = f32[64,64]{0,1:T(8,128)S(1)} fusion(f32[64,16384]{1,0:T(8,128)} %all-reduce.5.cloned.1.call-done, f32[8,8,128,128]{3,2,1,0:T(8,128)} %bitcast.37), kind=kOutput, calls=%fused_computation.21 | convolution fusion | flops 806354944 | bytes 8404992 | tf_op jit(solution)/shard_map/dot_general | solution.py:37
  269.0 555.0 %psum.31 = f32[64,64]{0,1:T(8,128)S(1)} all-reduce(f32[64,64]{0,1:T(8,128)S(1)} %fusion.6), channel_id=1, replica_groups=mesh['lon'=16,'lat'=8,'tm'=2] {'lon','lat'}, use_global_device_ids=true, to_apply=%region_3.4 | all-reduce | flops 4096 | bytes 32768 | tf_op jit(solution)/shard_map/psum | solution.py:69
  824.0 6.1 fusion.5
  830.1 2.8 copy.121
  833.0 5.8 cholesky.16
  840.3 4.9 custom-call.7
  845.2 8.4 fusion
  853.6 4.4 copy.110
  (51 shorter events, 16.9 us)
Async XLA Ops:
  7.2 247.9 %all-reduce.5.cloned.1.call-start = ((), (), s32[]{:S(2)}) async-start(), calls=%async_computation | async-start | bytes 8388608 | tf_op jit(solution)/shard_map/psum | solution.py:68
  8.4 9.4 %collective-permute-start.1 = (f32[8,8,1,128]{3,1,2,0:T(8,128)S(1)}, f32[8,8,1,128]{3,1,2,0:T(8,128)S(1)}, u32[]{:S(2)}, u32[]{:S(2)}) collective-permute-start(f32[8,8,1,128]{3,1,2,0:T(8,128)S(1)} %get-tuple-element.23), channel_id=1, source_target_pairs={{2,0},{4,2},{6,4},{8,6},{10,8},{12,10},{14,12},{3,1},{5,3},{7,5},{... | collective-permute-start | bytes 98312 | tf_op jit(solution)/shard_map/ppermute | solution.py:29
  9.7 10.7 %collective-permute-start = (f32[8,8,1,128]{3,1,2,0:T(8,128)S(1)}, f32[8,8,1,128]{3,1,2,0:T(8,128)S(1)}, u32[]{:S(2)}, u32[]{:S(2)}) collective-permute-start(f32[8,8,1,128]{3,1,2,0:T(8,128)S(1)} %get-tuple-element.22), channel_id=1, source_target_pairs={{0,2},{2,4},{4,6},{6,8},{8,10},{10,12},{12,14},{1,3},{3,5},{5,7},{... | collective-permute-start | bytes 98312 | tf_op jit(solution)/shard_map/ppermute | solution.py:27
  30.0 2.0 copy-start.1
  32.0 6.7 collective-permute-start.2
  32.0 7.2 collective-permute-start.3
  41.6 5.4 collective-permute-start.4
  45.5 5.8 collective-permute-start.5
  52.0 3.1 collective-permute-start.7
  54.0 6.0 collective-permute-start.6
  62.4 6.4 collective-permute-start.8
  67.3 5.9 collective-permute-start.9
  73.9 1.7 collective-permute-start.11
  74.5 5.5 collective-permute-start.10
  81.6 2.2 copy-start
  133.4 5.1 copy-start.2
Sparse Core Ops, SparseCore 0:
  138.6 116.3 all-reduce.4
